TPU v7x, 32 devices: a whole 2x2x4 slice. The times are simulated.
32 devices in a mesh: rep: 16 (over z, y, core), fsdp: 2 (over x).
Axes of the slice: x: 2, y: 2, z: 4, core: 2. Of those that a mesh axis runs over, the one named last changes fastest.
Arguments:
- activations: bfloat16 [4096, 8192], P(('rep', 'fsdp')), may hold values from -7.75 to 7.75
- upstream: bfloat16 [4096, 512], P(('rep', 'fsdp')), may hold values from -0.484375 to 0.484375
- q_start: float32 [2, 4, 512], P('fsdp'), may hold values from -6 to 6
Outputs:
- error_feedback: bfloat16 [16, 8192, 512], P('rep', 'fsdp')
- p_basis: float32 [2, 4, 4096], P('fsdp')
- q_factor: float32 [2, 4, 512], P('fsdp')
All inputs are finite; a program needn't handle non-finite values.
Results may differ from a plain program's by a relative error of at most 0.015.
Values may be sent and summed in bfloat16 or wider, within the bound.
A program may use at most 64 MiB of HBM per device.

v0:
```python
import jax
import jax.numpy as jnp
from jax import lax
from jax.sharding import PartitionSpec as P


def contract_tokens(left, right):
    return lax.dot_general(
        left, right, (((0,), (0,)), ((), ())), preferred_element_type=jnp.float32
    )


def rounded(term):
    short = lax.optimization_barrier(term.astype(jnp.bfloat16))
    return short.astype(jnp.float32)


def on_device(activations, upstream, q_start):
    high = lax.Precision.HIGHEST
    groups = lax.axis_size("fsdp")
    replicas = lax.axis_size("rep")
    tok_rows = activations.shape[0]
    shard_rows = activations.shape[1] // groups
    columns = lax.all_to_all(activations, "fsdp", split_axis=1, concat_axis=0, tiled=True)
    cotangent_all = lax.all_gather(upstream, "fsdp", axis=0, tiled=True)
    shard = jnp.zeros((shard_rows, upstream.shape[1]), jnp.float32)
    for source in range(groups):
        left = columns[source * tok_rows : (source + 1) * tok_rows]
        right = cotangent_all[source * tok_rows : (source + 1) * tok_rows]
        shard = shard + rounded(contract_tokens(left, right))
    q_local = q_start[0]
    left_local = lax.dot_general(
        q_local, shard, (((1,), (1,)), ((), ())), precision=high, preferred_element_type=jnp.float32
    )
    p_sum = lax.psum(left_local, "rep")
    basis = []
    for i in range(p_sum.shape[0]):
        vector = p_sum[i]
        for earlier in basis:
            vector = vector - jnp.sum(vector * earlier) * earlier
        basis.append(vector / jnp.sqrt(jnp.sum(vector * vector) + 1e-06))
    p_basis = jnp.stack(basis)
    right_local = jnp.dot(p_basis, shard, precision=high)
    q_factor = lax.psum(right_local, "rep")
    approx = lax.dot_general(
        p_basis,
        q_factor / replicas,
        (((0,), (0,)), ((), ())),
        precision=high,
        preferred_element_type=jnp.float32,
    )
    error_feedback = (shard - approx).astype(jnp.bfloat16)
    return (error_feedback[None], p_basis[None], q_factor[None])


def solution(mesh):
    in_specs = (P(("rep", "fsdp"), None), P(("rep", "fsdp"), None), P("fsdp", None, None))
    out_specs = (P("rep", "fsdp", None), P("fsdp", None, None), P("fsdp", None, None))
    return jax.shard_map(
        on_device, mesh=mesh, in_specs=in_specs, out_specs=out_specs, check_vma=False
    )
```

profile of v0, /device:TPU:0, one launch (start us, length us, event | category | flops | bytes accessed | tf_op | source)
XLA Modules:
  0.0 222.7 jit_solution(16569028851342070702)
XLA Ops:
  7.2 0.0 copy-start
  7.2 0.0 copy-start.3
  7.2 4.1 %copy.6 = bf16[128,8192]{0,1:T(8,128)(2,1)} copy(bf16[128,8192]{1,0:T(8,128)(2,1)} %param.3) | data formatting | bytes 4194304 | tf_op args[0]
  11.3 4.2 %all-to-all-start = ((bf16[128,2,4096]{0,2,1:T(8,128)(2,1)}), bf16[128,2,4096]{0,2,1:T(8,128)(2,1)S(1)}, u32[]{:S(2)}, u32[]{:S(2)}) async-start(bf16[128,2,4096]{0,2,1:T(8,128)(2,1)} %bitcast.26), calls=%async_computation | async-start | bytes 4194304 | tf_op jit(solution)/shard_map/all_to_all | solution.py:24
  15.5 0.0 all-reduce.2.cloned.1.call-start
  15.5 0.0 copy-done.3
  15.5 28.7 %all_gather.3 = bf16[256,512]{1,0:T(8,128)(2,1)S(1)} all-gather(bf16[128,512]{1,0:T(8,128)(2,1)S(1)} %copy-done.3), channel_id=1, replica_groups=mesh['rep'=16,'fsdp'=2] {'fsdp'}, dimensions={0}, use_global_device_ids=true | all-gather | bytes 393216 | tf_op jit(solution)/shard_map/all_gather | solution.py:25
  44.2 0.0 all-to-all-done
  44.2 1.2 convolution_convert_fusion
  45.4 0.0 copy-start.1
  45.5 1.2 convolution_convert_fusion.1
  46.7 0.8 copy-done.1
  47.5 0.0 copy-start.2
  47.5 1.9 copy-done.2
  49.4 0.0 copy-done
  49.4 8.4 %fusion.3 = f32[4,4096]{1,0:T(4,128)} fusion(bf16[4096,512]{1,0:T(8,128)(2,1)S(1)} %convolution_convert_fusion, bf16[4096,512]{1,0:T(8,128)(2,1)S(1)} %convolution_convert_fusion.1, f32[1,4,512]{2,1,0:T(4,128)S(1)} %copy-done), kind=kOutput, calls=%fused_computation.7 | convolution fusion | flops 106954752 | bytes 8462336 | tf_op jit(solution)/shard_map/dot_general | solution.py:32
  57.8 0.0 all-reduce.2.cloned.1.call-update
  57.9 87.0 %all-reduce.2.cloned.1.call-done = f32[4,4096]{1,0:T(4,128)} async-done(((f32[4,4096]{1,0:T(4,128)}), f32[4,4096]{1,0:T(4,128)}) %all-reduce.2.cloned.1.call-update) | async-done | bytes 65552 | tf_op jit(solution)/shard_map/psum | solution.py:35
  144.8 1.5 multiply_reduce_fusion.9
  147.0 1.1 fusion.11
  148.1 0.6 multiply_reduce_fusion.8
  148.7 1.3 multiply_reduce_fusion.3
  150.7 2.5 %multiply_reduce_fusion.2 = (f32[]{:T(128)}, f32[]{:T(128)}, f32[4096]{0:T(1024)S(1)}) fusion(f32[4096]{0:T(1024)S(1)} %bitcast.36, f32[4096]{0:T(1024)S(1)} %bitcast.29, f32[]{:T(128)} %get-tuple-element.5, f32[4096]{0:T(1024)S(1)} %bitcast.39, f32[]{:T(128)} %get-tuple-element.6, f32[]{:T(128)S(6)} %sqrt.13, f32[4096]{0:T(1024)S(1)} %bitcast.34, ...), kind=kLoop, calls=%fused_computation.17 | loop fusion | flops 45054 | bytes 81944 | tf_op jit(solution)/shard_map/reduce_sum | solution.py:40
  153.2 1.8 multiply_reduce_fusion.4
  155.7 1.9 multiply_reduce_fusion.1
  157.6 1.3 multiply_reduce_fusion
  159.5 4.8 %subtract_divide_fusion = (f32[1,4096]{1,0:T(1,128)S(1)}, f32[1,4096]{1,0:T(1,128)S(1)}, f32[1,4096]{1,0:T(1,128)S(1)}) fusion(f32[1,4096]{1,0:T(1,128)S(1)} %get-tuple-element.17, f32[]{:T(128)S(6)} %sqrt.15, f32[]{:T(128)} %get-tuple-element.11, f32[]{:T(128)} %get-tuple-element.3, f32[]{:T(128)} %get-tuple-element.5, ...), kind=kLoop, calls=%fused_computation.14 | loop fusion | flops 61440 | bytes 114724 | tf_op jit(solution)/shard_map/div | solution.py:41
  164.3 7.1 %fusion = f32[4,512]{1,0:T(4,128)S(1)} fusion(bf16[4096,512]{1,0:T(8,128)(2,1)} %copy-done.1, bf16[4096,512]{1,0:T(8,128)(2,1)} %copy-done.2, f32[1,4096]{1,0:T(1,128)S(1)} %get-tuple-element.8, f32[1,4096]{1,0:T(1,128)S(1)} %get-tuple-element.9, f32[1,4096]{1,0:T(1,128)S(1)} %get-tuple-element.10, f32[1,4096]{1,0:T(1,128)S(1)} %get-tuple-element.17), kind=kOutput, calls=%fused_computation.2 | convolution fusion | flops 107003904 | bytes 8462336 | tf_op jit(solution)/shard_map/dot_general | solution.py:43
  171.4 0.7 fusion.10
  172.1 32.4 %psum.15 = f32[4,512]{1,0:T(4,128)S(1)} all-reduce(f32[4,512]{1,0:T(4,128)S(1)} %fusion), channel_id=1, replica_groups=mesh['rep'=16,'fsdp'=2] {'rep'}, use_global_device_ids=true, to_apply=%region_11.0 | all-reduce | flops 2048 | bytes 16384 | tf_op jit(solution)/shard_map/psum | solution.py:44
  204.6 0.0 copy-start.4
  204.6 11.3 %fusion.2 = bf16[1,4096,512]{2,1,0:T(8,128)(2,1)} fusion(bf16[4096,512]{1,0:T(8,128)(2,1)} %copy-done.1, bf16[4096,512]{1,0:T(8,128)(2,1)} %copy-done.2, f32[4,512]{1,0:T(4,128)S(1)} %psum.15, f32[1,4096]{1,0:T(1,128)S(1)} %get-tuple-element.8, f32[1,4096]{1,0:T(1,128)S(1)} %get-tuple-element.9, f32[1,4096]{1,0:T(1,128)S(1)} %get-tuple-element.10, ...), kind=kOutput, calls=%fused_computation.6 | convolution fusion | flops 111200256 | bytes 12656640 | tf_op jit(solution)/shard_map/dot_general | solution.py:45
  215.9 0.0 copy-done.4
Async XLA Ops:
  7.2 42.2 %copy-start = (f32[1,4,512]{2,1,0:T(4,128)S(1)}, f32[1,4,512]{2,1,0:T(4,128)}, u32[]{:S(2)}) copy-start(f32[1,4,512]{2,1,0:T(4,128)} %param.5) | copy-start | bytes 24580
  7.2 8.4 %copy-start.3 = (bf16[128,512]{1,0:T(8,128)(2,1)S(1)}, bf16[128,512]{1,0:T(8,128)(2,1)}, u32[]{:S(2)}) copy-start(bf16[128,512]{1,0:T(8,128)(2,1)} %param.4) | copy-start | bytes 393220
  11.3 32.9 %all-to-all-start = ((bf16[128,2,4096]{0,2,1:T(8,128)(2,1)}), bf16[128,2,4096]{0,2,1:T(8,128)(2,1)S(1)}, u32[]{:S(2)}, u32[]{:S(2)}) async-start(bf16[128,2,4096]{0,2,1:T(8,128)(2,1)} %bitcast.26), calls=%async_computation | async-start | bytes 4194304 | tf_op jit(solution)/shard_map/all_to_all | solution.py:24
  15.5 129.3 %all-reduce.2.cloned.1.call-start = ((), (), s32[]{:S(2)}) async-start(), calls=%async_computation.1 | async-start | bytes 131072 | tf_op jit(solution)/shard_map/psum | solution.py:35
  45.4 2.0 copy-start.1
  47.5 1.9 copy-start.2
  204.6 11.3 %copy-start.4 = (f32[4,512]{1,0:T(4,128)}, f32[4,512]{1,0:T(4,128)S(1)}, u32[]{:S(2)}) copy-start(f32[4,512]{1,0:T(4,128)S(1)} %psum.15) | copy-start | bytes 24580
Sparse Core Ops, SparseCore 0:
  58.0 86.7 all-reduce.1
where the time goes:
time: 223 us
  waiting for transfers between devices  87 us (39%)
  blocking collectives  61.1 us (27%)
  matrix products  29.3 us (13%)
  other arithmetic  17.4 us (8%)
  between operations  16.8 us (8%)
  local copies, waits for them, and re-layouts  6.82 us (3%)
  starting transfers between devices  4.24 us (2%)
    psum x1, waiting for transfers between devices, on_device(): p_sum = lax.psum(left_local, 'rep')  87 us
    psum x1, blocking collectives, on_device(): q_factor = lax.psum(right_local, 'rep')  32.4 us
    all_gather x1, blocking collectives, on_device(): cotangent_all = lax.all_gather(upstream, 'fsdp', axis=0, tiled=True)  28.7 us
    dot_general x1, matrix products, on_device(): lax.dot_general(p_basis, q_factor / replicas, (((0,), (0,)), ((), ())), p...  11.3 us
    dot_general x1, matrix products, on_device(): lax.dot_general(q_local, shard, (((1,), (1,)), ((), ())), precision=high,...  8.44 us
    dot_general x1, matrix products, on_device(): right_local = jnp.dot(p_basis, shard, precision=high)  7.14 us
    unnamed x11, local copies, waits for them, and re-layouts  6.82 us
    reduce_sum x4, other arithmetic, on_device(): vector = vector - jnp.sum(vector * earlier) * earlier  6.39 us
  transfers between devices with their start and end apart: 2, of which 1 were waited for; matrix products, arithmetic and copies ran while one was open for 0% of the time, Pallas kernels for 0%

commit v1 on v0

v1 whole, which is shorter than its diff:
```python
import functools
import math

import jax
import jax.numpy as jnp
from jax import lax
from jax.experimental import pallas as pl
from jax.experimental.pallas import tpu as pltpu
from jax.sharding import PartitionSpec as P

MESH = pl.DeviceIdType.MESH
BF16 = jnp.bfloat16
F32 = jnp.float32


def two_terms(x):
    high = x.astype(BF16).astype(F32)
    return jnp.concatenate([high, x - high], axis=0).astype(BF16)


def folded(y):
    half = y.shape[0] // 2
    return y[:half] + y[half:]


def dot(a, b):
    return lax.dot_general(a, b, (((1,), (0,)), ((), ())), preferred_element_type=F32)


def dot_nt(a, b):
    return lax.dot_general(a, b, (((1,), (1,)), ((), ())), preferred_element_type=F32)


def exchange_kernel(
    cfg, act_hbm, up, q0, left_all, up_all, p_out, q_out,
    act, left, q_in, pc, pc_in, ps, rs_in, pfull, p_in, cc, c_in, g_in,
    local_sem, q_s, q_r, u_s, u_r, pc_s, pc_r, b_s, b_r, rs_s, rs_r, ag_s, ag_r,
    p_s, p_r, c_s, c_r, g_s, g_r,
):
    reps, groups, chunks, part1, part2, parts = cfg
    me = lax.axis_index("rep")
    mf = lax.axis_index("fsdp")
    tok, width = act.shape
    rows = width // groups
    stride = reps // chunks
    piece = rows // parts
    rank = q0.shape[1]
    cw = rows // chunks

    barrier = pltpu.get_barrier_semaphore()
    load = pltpu.make_async_copy(act_hbm, act, local_sem.at[0])
    load.start()

    def greet(d, _):
        pl.semaphore_signal(barrier, inc=1, device_id={"rep": lax.rem(me + d, reps)}, device_id_type=MESH)
        return 0

    for d in range(1, groups):
        pl.semaphore_signal(barrier, inc=1, device_id={"fsdp": lax.rem(mf + d, groups)}, device_id_type=MESH)
    lax.fori_loop(1, reps, greet, 0)
    keep_up = pltpu.make_async_copy(up, up_all.at[pl.ds(pl.multiple_of(mf * tok, tok), tok)], local_sem.at[1])
    keep_up.start()

    def to_group(d, src, dst, s, r):
        return pltpu.make_async_remote_copy(
            src_ref=src, dst_ref=dst, send_sem=s, recv_sem=r,
            device_id={"fsdp": lax.rem(mf + d, groups)}, device_id_type=MESH,
        )

    def to_rep(j, src, dst, s, r):
        return pltpu.make_async_remote_copy(
            src_ref=src, dst_ref=dst, send_sem=s, recv_sem=r,
            device_id={"rep": j}, device_id_type=MESH,
        )

    qs, us, bulk, pcs, pss, cs = [], [], [], [], [], []
    pl.semaphore_wait(barrier, reps - 1 + groups - 1)
    for d in range(1, groups):
        c = to_group(d, q0.at[0], q_in.at[d - 1], q_s.at[d - 1], q_r.at[d - 1])
        c.start()
        qs.append(c)
    for d in range(1, groups):
        c = to_group(
            d, up, up_all.at[pl.ds(pl.multiple_of(mf * tok, tok), tok)], u_s.at[d - 1], u_r.at[d - 1]
        )
        c.start()
        us.append(c)

    upv = up[...]
    load.wait()

    def columns(g):
        return pl.ds(pl.multiple_of(g * rows, rows), rows)

    def turn(i, _):
        at = pl.ds(pl.multiple_of(i * piece, piece), piece)
        left[at, :] = act[:, at].T
        return 0

    def project(qv, g):
        w = folded(dot_nt(two_terms(qv), upv))
        return folded(dot(two_terms(w), act[:, columns(g)]))

    for d in range(1, groups):
        qs[groups - d - 1].wait_recv()
        val = project(q_in[groups - d - 1], lax.rem(mf + d, groups))
        for c in range(chunks):
            pc[d - 1, c] = val[:, c * cw:(c + 1) * cw]
        cp = to_group(d, pc.at[d - 1], pc_in.at[d - 1], pc_s.at[d - 1], pc_r.at[d - 1])
        cp.start()
        pcs.append(cp)
    lax.fori_loop(0, groups * parts, turn, 0)

    for d in range(1, groups):
        g = lax.rem(mf + d, groups)
        row = []
        for k in range(parts):
            row.append(
                to_group(
                    d,
                    left.at[pl.ds(pl.multiple_of(g * rows + k * piece, piece), piece)],
                    left_all.at[pl.ds(k * piece, piece), pl.ds(pl.multiple_of(mf * tok, tok), tok)],
                    b_s.at[d - 1, k],
                    b_r.at[d - 1, k],
                )
            )
        bulk.append(row)

    def send_bulk(a, b):
        for k in range(a, b):
            for row in bulk:
                row[k].start()

    send_bulk(0, part1)
    keep_left = pltpu.make_async_copy(
        left.at[columns(mf)], left_all.at[:, pl.ds(pl.multiple_of(mf * tok, tok), tok)], local_sem.at[2]
    )
    keep_left.start()

    own = project(q0[0], mf)
    for c in range(chunks):
        ps[c] = own[:, c * cw:(c + 1) * cw]
    total = ps[...]
    for d in range(1, groups):
        pcs[d - 1].wait_recv()
        total = total + pc_in[d - 1]
    ps[...] = total

    mine = me // stride
    owner = lax.rem(me, stride) == 0

    def rs_copy(c):
        return to_rep(c * stride, ps.at[c], rs_in.at[me], rs_s.at[c], rs_r.at[me])

    def rs_from(j):
        return to_rep(j, rs_in.at[j], rs_in.at[j], rs_s.at[0], rs_r.at[j])

    def rs_send(d, _):
        c = lax.rem(mine + d, chunks)
        rs_copy(c).start()
        return 0

    def rs_done(d, _):
        c = lax.rem(mine + d, chunks)
        rs_copy(c).wait_send()
        return 0

    def ag_copy(j):
        return to_rep(j, pfull.at[mine], pfull.at[mine], ag_s.at[j], ag_r.at[mine])

    def ag_from(c):
        return to_rep(c * stride, pfull.at[c], pfull.at[c], ag_s.at[0], ag_r.at[c])

    lax.fori_loop(1, chunks, rs_send, 0)
    if stride > 1:
        @pl.when(jnp.logical_not(owner))
        def _():
            rs_copy(mine).start()

    def reduce_mine():
        rs_in[me] = ps[mine]

        def arrive(d, _):
            rs_from(lax.rem(me + d, reps)).wait_recv()
            return 0

        lax.fori_loop(1, reps, arrive, 0)
        pfull[mine] = jnp.sum(rs_in[...], axis=0)

        def share(d, _):
            ag_copy(lax.rem(me + d, reps)).start()
            return 0

        lax.fori_loop(1, reps, share, 0)

    def gather(d, _):
        ag_from(lax.rem(mine + d, chunks)).wait_recv()
        return 0

    if stride > 1:
        pl.when(owner)(reduce_mine)

        @pl.when(jnp.logical_not(owner))
        def _():
            ag_from(mine).wait_recv()
    else:
        reduce_mine()
    lax.fori_loop(1, chunks, gather, 0)

    v = pfull[...]
    row_at = lax.broadcasted_iota(jnp.int32, v.shape, 1)
    for i in range(rank):
        lead = v[:, i:i + 1, :]
        dots = jnp.sum(jnp.sum(v * lead, axis=0, keepdims=True), axis=2, keepdims=True)
        inv = lax.rsqrt(dots[:, i:i + 1, :] + 1e-06)
        unit = lead * inv
        v = jnp.where(row_at > i, v - (dots * inv) * unit, jnp.where(row_at == i, unit, v))
    for c in range(chunks):
        p_out[:, c * cw:(c + 1) * cw] = v[c]
    for d in range(1, groups):
        cp = to_group(d, p_out, p_in.at[d - 1], p_s.at[d - 1], p_r.at[d - 1])
        cp.start()
        pss.append(cp)
    send_bulk(part1, part2)

    def back(pv, g):
        t = folded(dot(two_terms(pv), left[columns(g), :]))
        return folded(dot(two_terms(t), upv))

    c_own = back(p_out[...], mf)
    for d in range(1, groups):
        pss[groups - d - 1].wait_recv()
        cc[d - 1] = back(p_in[groups - d - 1], lax.rem(mf + d, groups))
        cp = to_group(d, cc.at[d - 1], c_in.at[d - 1], c_s.at[d - 1], c_r.at[d - 1])
        cp.start()
        cs.append(cp)
    send_bulk(part2, parts)
    for d in range(1, groups):
        cs[d - 1].wait_recv()
        c_own = c_own + c_in[d - 1]
    g_in[me] = c_own

    def g_copy(j):
        return to_rep(j, g_in.at[me], g_in.at[me], g_s.at[j], g_r.at[me])

    def g_send(d, _):
        g_copy(lax.rem(me + d, reps)).start()
        return 0

    def g_arrive(d, _):
        j = lax.rem(me + d, reps)
        to_rep(j, g_in.at[j], g_in.at[j], g_s.at[0], g_r.at[j]).wait_recv()
        return 0

    def g_done(d, _):
        g_copy(lax.rem(me + d, reps)).wait_send()
        return 0

    def ag_done(d, _):
        ag_copy(lax.rem(me + d, reps)).wait_send()
        return 0

    lax.fori_loop(1, reps, g_send, 0)
    lax.fori_loop(1, reps, g_arrive, 0)
    q_out[...] = jnp.sum(g_in[...], axis=0)

    lax.fori_loop(1, chunks, rs_done, 0)
    if stride > 1:
        @pl.when(jnp.logical_not(owner))
        def _():
            rs_copy(mine).wait_send()

        @pl.when(owner)
        def _():
            lax.fori_loop(1, reps, ag_done, 0)
    else:
        lax.fori_loop(1, reps, ag_done, 0)
    lax.fori_loop(1, reps, g_done, 0)
    for c in qs + pcs + pss + cs:
        c.wait_send()
    keep_up.wait()
    keep_left.wait()
    for c in us:
        c.wait()
    for k in range(parts):
        for row in bulk:
            row[k].wait()


def residual_kernel(reps, left, up, p, q, err, p_out, q_out):
    pv, qv = p[...], q[...]
    q_out[0] = qv
    p_out[0] = pv
    scaled = qv * (-1.0 / reps) if reps & (reps - 1) == 0 else -(qv / reps)
    ph = pv.astype(BF16).astype(F32)
    qh = scaled.astype(BF16).astype(F32)
    pst = jnp.concatenate([ph, pv - ph, ph, pv - ph], axis=0).astype(BF16)
    qst = jnp.concatenate([qh, qh, scaled - qh, scaled - qh], axis=0).astype(BF16)
    low = lax.dot_general(pst, qst, (((0,), (0,)), ((), ())), preferred_element_type=F32)
    err[0] = (dot(left[...], up[...]) + low).astype(BF16)


def on_device(activations, upstream, q_start):
    reps = lax.axis_size("rep")
    groups = lax.axis_size("fsdp")
    tok, width = activations.shape
    kvw = upstream.shape[1]
    rank = q_start.shape[1]
    rows = width // groups
    chunks = math.gcd(reps, rows // 128)
    cw = rows // chunks
    parts = 8
    cfg = (reps, groups, chunks, 3, 5, parts)
    vm = pl.BlockSpec(memory_space=pltpu.VMEM)
    hbm = pl.BlockSpec(memory_space=pl.ANY)
    dma = pltpu.SemaphoreType.DMA
    peers = groups - 1
    left_all, up_all, p_basis, q_factor = pl.pallas_call(
        functools.partial(exchange_kernel, cfg),
        out_shape=(
            jax.ShapeDtypeStruct((rows, groups * tok), BF16),
            jax.ShapeDtypeStruct((groups * tok, kvw), BF16),
            jax.ShapeDtypeStruct((rank, rows), F32),
            jax.ShapeDtypeStruct((rank, kvw), F32),
        ),
        in_specs=[hbm, vm, vm],
        out_specs=(hbm, hbm, vm, vm),
        scratch_shapes=[
            pltpu.VMEM((tok, width), BF16),
            pltpu.VMEM((width, tok), BF16),
            pltpu.VMEM((peers, rank, kvw), F32),
            pltpu.VMEM((peers, chunks, rank, cw), F32),
            pltpu.VMEM((peers, chunks, rank, cw), F32),
            pltpu.VMEM((chunks, rank, cw), F32),
            pltpu.VMEM((reps, rank, cw), F32),
            pltpu.VMEM((chunks, rank, cw), F32),
            pltpu.VMEM((peers, rank, rows), F32),
            pltpu.VMEM((peers, rank, kvw), F32),
            pltpu.VMEM((peers, rank, kvw), F32),
            pltpu.VMEM((reps, rank, kvw), F32),
            dma((3,)),
            dma((peers,)), dma((peers,)),
            dma((peers,)), dma((peers,)),
            dma((peers,)), dma((peers,)),
            dma((peers, parts)), dma((peers, parts)),
            dma((chunks,)), dma((reps,)),
            dma((reps,)), dma((chunks,)),
            dma((peers,)), dma((peers,)),
            dma((peers,)), dma((peers,)),
            dma((reps,)), dma((reps,)),
        ],
        compiler_params=pltpu.CompilerParams(collective_id=0, has_side_effects=True),
        name="exchange",
    )(activations, upstream, q_start)
    step = rows // 8
    return pl.pallas_call(
        functools.partial(residual_kernel, reps),
        grid=(8,),
        out_shape=(
            jax.ShapeDtypeStruct((1, rows, kvw), BF16),
            jax.ShapeDtypeStruct((1, rank, rows), F32),
            jax.ShapeDtypeStruct((1, rank, kvw), F32),
        ),
        in_specs=[
            pl.BlockSpec((step, groups * tok), lambda i: (i, 0)),
            pl.BlockSpec((groups * tok, kvw), lambda i: (0, 0)),
            pl.BlockSpec((rank, step), lambda i: (0, i)),
            pl.BlockSpec((rank, kvw), lambda i: (0, 0)),
        ],
        out_specs=(
            pl.BlockSpec((1, step, kvw), lambda i: (0, i, 0)),
            pl.BlockSpec((1, rank, step), lambda i: (0, 0, i)),
            pl.BlockSpec((1, rank, kvw), lambda i: (0, 0, 0)),
        ),
        name="residual",
    )(left_all, up_all, p_basis, q_factor)


def solution(mesh):
    in_specs = (P(("rep", "fsdp"), None), P(("rep", "fsdp"), None), P("fsdp", None, None))
    out_specs = (P("rep", "fsdp", None), P("fsdp", None, None), P("fsdp", None, None))
    return jax.shard_map(
        on_device, mesh=mesh, in_specs=in_specs, out_specs=out_specs, check_vma=False
    )
```

time: 223 us -> 51.8 us (0.23)
  waiting for transfers between devices: 87 us -> 0 us
  blocking collectives: 61.1 us -> 0 us
  Pallas kernels: 0 us -> 50.9 us
  matrix products: 29.3 us -> 0 us
  other arithmetic: 17.4 us -> 0 us
  between operations: 16.8 us -> 0.64 us
  local copies, waits for them, and re-layouts: 6.82 us -> 0 us
  starting transfers between devices: 4.24 us -> 0 us
    psum x1 -> x0, waiting for transfers between devices: 87 us -> none  [on_device(): p_sum = lax.psum(left_local, 'rep')]
    pallas_call x0 -> x2, Pallas kernels: none -> 50.9 us  [the longest x1 43 us: on_device(): pl.pallas_call(functools.partial(exchange_kernel, cfg), out_shape=(jax.Sh...]
    psum x1 -> x0, blocking collectives: 32.4 us -> none  [on_device(): q_factor = lax.psum(right_local, 'rep')]
    dot_general x5 -> x0, matrix products: 29.3 us -> none  [the longest x1 11.3 us: on_device(): lax.dot_general(p_basis, q_factor / replicas, (((0,), (0,)), ((), ())), p...]
    all_gather x1 -> x0, blocking collectives: 28.7 us -> none  [on_device(): cotangent_all = lax.all_gather(upstream, 'fsdp', axis=0, tiled=True)]
    reduce_sum x7 -> x0, other arithmetic: 10.9 us -> none  [the longest x4 6.39 us: on_device(): vector = vector - jnp.sum(vector * earlier) * earlier]
    unnamed x11 -> x0, local copies, waits for them, and re-layouts: 6.82 us -> none
    div x1 -> x0, other arithmetic: 4.8 us -> none  [on_device(): basis.append(vector / jnp.sqrt(jnp.sum(vector * vector) + 1e-06))]
  transfers between devices with their start and end apart: 2 -> 0, of which waited for: 1 -> 0; matrix products, arithmetic and copies ran while one was open for 0% -> 0% of each run, Pallas kernels for 0% -> 0%
where the time goes in v1:
time: 51.8 us; the launch traced here: 51.5 us
  Pallas kernels  50.9 us (98%)
  between operations  0.64 us (1%)
    pallas_call x1, Pallas kernels, on_device(): pl.pallas_call(functools.partial(exchange_kernel, cfg), out_shape=(jax.Sh...  43 us
    pallas_call x1, Pallas kernels, on_device(): pl.pallas_call(functools.partial(residual_kernel, reps), grid=(8,), out_s...  7.87 us

profile of v1, /device:TPU:0, one launch (start us, length us, event | category | flops | bytes accessed | tf_op | source)
XLA Modules:
  0.0 51.5 jit_solution(18001613414413436212)
XLA Ops:
  0.6 43.0 %exchange.1 = (bf16[4096,256]{1,0:T(8,128)(2,1)}, bf16[256,512]{1,0:T(8,128)(2,1)}, f32[4,4096]{1,0:T(4,128)}, f32[4,512]{1,0:T(4,128)}) custom-call(bf16[128,8192]{1,0:T(8,128)(2,1)} %act_hbm.1, bf16[128,512]{1,0:T(8,128)(2,1)} %up.1, f32[1,4,512]{2,1,0:T(4,128)} %q0.1), custom_call_target="tpu_custom_call" | custom-call | tf_op jit(solution)/shard_map/exchange/pallas_call | solution.py:318
  43.6 7.9 %residual.1 = (bf16[1,4096,512]{2,1,0:T(8,128)(2,1)}, f32[1,4,4096]{2,1,0:T(4,128)}, f32[1,4,512]{2,1,0:T(4,128)}) custom-call(bf16[4096,256]{1,0:T(8,128)(2,1)} %get-tuple-element.7.left, bf16[256,512]{1,0:T(8,128)(2,1)} %get-tuple-element.8.up, f32[4,4096]{1,0:T(4,128)} %get-tuple-element.9.p, f32[4,512]{1,0:T(4,128)} %get-tuple-element.10.q), custom_call_target="tpu_custom_call" | custom-call | tf_op jit(solution)/shard_map/residual/pallas_call | solution.py:356

commit v2 on v0

v2 whole, which is shorter than its diff:
```python
import functools
import math

import jax
import jax.numpy as jnp
from jax import lax
from jax.experimental import pallas as pl
from jax.experimental.pallas import tpu as pltpu
from jax.sharding import PartitionSpec as P

MESH = pl.DeviceIdType.MESH
BF16 = jnp.bfloat16
F32 = jnp.float32


def two_terms(x):
    high = x.astype(BF16).astype(F32)
    return jnp.concatenate([high, x - high], axis=0).astype(BF16)


def folded(y):
    half = y.shape[0] // 2
    return y[:half] + y[half:]


def dot(a, b):
    return lax.dot_general(a, b, (((1,), (0,)), ((), ())), preferred_element_type=F32)


def dot_nt(a, b):
    return lax.dot_general(a, b, (((1,), (1,)), ((), ())), preferred_element_type=F32)


def exchange_kernel(
    cfg, act_hbm, up, q0, left_all, up_all, p_out, q_out,
    act, left, q_in, pc, rs_in, pfull, p_flat, cc, c_in, g_in,
    local_sem, q_s, q_r, u_s, u_r, b_s, b_r, rs_s, rs_r, ag_s, ag_r, c_s, c_r, g_s, g_r,
):
    reps, groups, chunks, part1, part2, parts = cfg
    me = lax.axis_index("rep")
    mf = lax.axis_index("fsdp")
    tok, width = act.shape
    rows = width // groups
    stride = reps // chunks
    piece = rows // parts
    rank = q0.shape[1]
    cw = rows // chunks

    def ahead(d):
        return lax.rem(mf + d, groups)

    def remote(rep, group, src, dst, s, r):
        return pltpu.make_async_remote_copy(
            src_ref=src, dst_ref=dst, send_sem=s, recv_sem=r,
            device_id={"rep": rep, "fsdp": group}, device_id_type=MESH,
        )

    def loop(a, b, fn):
        def body(i, carry):
            fn(i)
            return carry

        lax.fori_loop(a, b, body, 0)

    load = pltpu.make_async_copy(act_hbm, act, local_sem.at[0])
    load.start()
    barrier = pltpu.get_barrier_semaphore()
    for f in range(groups):
        def greet(d):
            pl.semaphore_signal(
                barrier, inc=1, device_id={"rep": lax.rem(me + d, reps), "fsdp": ahead(f)},
                device_id_type=MESH,
            )

        loop(0 if f else 1, reps, greet)
    my_tokens = pl.ds(pl.multiple_of(mf * tok, tok), tok)
    keep_up = pltpu.make_async_copy(up, up_all.at[my_tokens], local_sem.at[1])
    keep_up.start()
    upv = up[...]

    def columns(g):
        return pl.ds(pl.multiple_of(g * rows, rows), rows)

    def project(qv, g):
        w = folded(dot_nt(two_terms(qv), upv))
        val = folded(dot(two_terms(w), act[:, columns(g)]))
        for c in range(chunks):
            pc[g, c] = val[:, c * cw:(c + 1) * cw]

    def turn(i):
        at = pl.ds(pl.multiple_of(i * piece, piece), piece)
        left[at, :] = act[:, at].T

    load.wait()
    project(q0[0], mf)
    loop(0, groups * parts, turn)
    keep_left = pltpu.make_async_copy(left.at[columns(mf)], left_all.at[:, my_tokens], local_sem.at[2])
    keep_left.start()
    pl.semaphore_wait(barrier, reps * groups - 1)

    qs, us, bulk, cs = [], [], [], []
    for d in range(1, groups):
        qs.append(remote(me, ahead(d), q0.at[0], q_in.at[d - 1], q_s.at[d - 1], q_r.at[d - 1]))
        qs[-1].start()
    for d in range(1, groups):
        us.append(remote(me, ahead(d), up, up_all.at[my_tokens], u_s.at[d - 1], u_r.at[d - 1]))
        us[-1].start()

    mine = me // stride
    owner = lax.rem(me, stride) == 0
    my_slot = mf * reps + me

    def rs_copy(g, c):
        return remote(c * stride, g, pc.at[g, c], rs_in.at[my_slot], rs_s.at[g, c], rs_r.at[my_slot])

    def rs_all(g, act_on, own_shard):
        if own_shard:
            loop(1, chunks, lambda d: act_on(rs_copy(g, lax.rem(mine + d, chunks))))
            if stride > 1:
                @pl.when(jnp.logical_not(owner))
                def _():
                    act_on(rs_copy(g, mine))
        else:
            loop(0, chunks, lambda d: act_on(rs_copy(g, lax.rem(mine + d, chunks))))

    rs_all(mf, lambda c: c.start(), True)
    for d in range(1, groups):
        qs[groups - d - 1].wait_recv()
        project(q_in[groups - d - 1], ahead(d))
        rs_all(ahead(d), lambda c: c.start(), False)

    for d in range(1, groups):
        bulk.append([
            remote(
                me, ahead(d),
                left.at[pl.ds(pl.multiple_of(ahead(d) * rows + k * piece, piece), piece)],
                left_all.at[pl.ds(k * piece, piece), my_tokens],
                b_s.at[d - 1, k], b_r.at[d - 1, k],
            )
            for k in range(parts)
        ])

    def send_bulk(a, b):
        for k in range(a, b):
            for row in bulk:
                row[k].start()

    send_bulk(0, part1)

    def ag_copy(rep, g):
        return remote(
            rep, g, pfull.at[mf, mine], pfull.at[mf, mine], ag_s.at[g * reps + rep], ag_r.at[mf * chunks + mine]
        )

    def ag_all(act_on):
        for d in list(range(1, groups)) + [0]:
            loop(0 if d else 1, reps, lambda i: act_on(ag_copy(lax.rem(me + i, reps), ahead(d))))

    def reduce_mine():
        rs_in[my_slot] = pc[mf, mine]

        def arrive(i):
            j = lax.rem(my_slot + i, reps * groups)
            remote(
                lax.rem(j, reps), j // reps, rs_in.at[j], rs_in.at[j], rs_s.at[0, 0], rs_r.at[j]
            ).wait_recv()

        loop(1, reps * groups, arrive)
        pfull[mf, mine] = jnp.sum(rs_in[...], axis=0)
        ag_all(lambda c: c.start())

    def gather(i):
        j = lax.rem(mf * chunks + mine + i, groups * chunks)
        g, c = j // chunks, lax.rem(j, chunks)
        remote(c * stride, g, pfull.at[g, c], pfull.at[g, c], ag_s.at[0], ag_r.at[j]).wait_recv()

    if stride > 1:
        pl.when(owner)(reduce_mine)
        pl.when(jnp.logical_not(owner))(lambda: gather(0))
    else:
        reduce_mine()
    send_bulk(part1, part2)
    loop(1, groups * chunks, gather)

    v = pfull[...]
    row_at = lax.broadcasted_iota(jnp.int32, v.shape, 2)
    for i in range(rank):
        lead = v[:, :, i:i + 1, :]
        dots = jnp.sum(jnp.sum(v * lead, axis=1, keepdims=True), axis=3, keepdims=True)
        inv = lax.rsqrt(dots[:, :, i:i + 1, :] + 1e-06)
        unit = lead * inv
        v = jnp.where(row_at > i, v - (dots * inv) * unit, jnp.where(row_at == i, unit, v))
    for g in range(groups):
        for c in range(chunks):
            p_flat[g, :, c * cw:(c + 1) * cw] = v[g, c]
        t = folded(dot(two_terms(p_flat[g]), left[g * rows:(g + 1) * rows, :]))
        cc[g] = folded(dot(two_terms(t), upv))
    for d in range(1, groups):
        g = ahead(d)
        cs.append(remote(me, g, cc.at[g], c_in.at[d - 1], c_s.at[d - 1], c_r.at[d - 1]))
        cs[-1].start()
    send_bulk(part2, parts)
    p_out[...] = p_flat[mf]
    total = cc[mf]
    for c, got in zip(cs, range(groups - 1)):
        c.wait_recv()
        total = total + c_in[got]
    g_in[me] = total

    def g_copy(i):
        j = lax.rem(me + i, reps)
        return remote(j, mf, g_in.at[me], g_in.at[me], g_s.at[j], g_r.at[me])

    def g_arrive(i):
        j = lax.rem(me + i, reps)
        remote(j, mf, g_in.at[j], g_in.at[j], g_s.at[0], g_r.at[j]).wait_recv()

    loop(1, reps, lambda i: g_copy(i).start())
    loop(1, reps, g_arrive)
    q_out[...] = jnp.sum(g_in[...], axis=0)

    for c in qs + cs:
        c.wait_send()
    for d in range(groups):
        rs_all(ahead(d), lambda c: c.wait_send(), d == 0)
    if stride > 1:
        pl.when(owner)(lambda: ag_all(lambda c: c.wait_send()))
    else:
        ag_all(lambda c: c.wait_send())
    loop(1, reps, lambda i: g_copy(i).wait_send())
    keep_up.wait()
    keep_left.wait()
    for c in us:
        c.wait()
    for k in range(parts):
        for row in bulk:
            row[k].wait()


def residual_kernel(
    reps, left_hbm, up_hbm, p_hbm, q_hbm, err, p_out, q_out, left, up, p, q, out, in_sem, left_sem, out_sem
):
    parts, step = left.shape[0], left.shape[1]
    small = [
        pltpu.make_async_copy(src, dst, in_sem.at[i])
        for i, (src, dst) in enumerate(((q_hbm, q), (p_hbm, p), (up_hbm, up)))
    ]
    loads = [
        pltpu.make_async_copy(left_hbm.at[pl.ds(k * step, step)], left.at[k], left_sem.at[k])
        for k in range(parts)
    ]
    for c in small + loads:
        c.start()
    for c in small:
        c.wait()
    stores = [
        pltpu.make_async_copy(p, p_out.at[0], out_sem.at[parts]),
        pltpu.make_async_copy(q, q_out.at[0], out_sem.at[parts + 1]),
    ]
    for c in stores:
        c.start()
    upv = up[...]
    scaled = -(q[...] / reps)
    qh = scaled.astype(BF16).astype(F32)
    qst = jnp.concatenate([qh, qh, scaled - qh, scaled - qh], axis=0).astype(BF16)
    for k in range(parts):
        pv = p[:, k * step:(k + 1) * step]
        ph = pv.astype(BF16).astype(F32)
        pst = jnp.concatenate([ph, pv - ph, ph, pv - ph], axis=0).astype(BF16)
        low = lax.dot_general(pst, qst, (((0,), (0,)), ((), ())), preferred_element_type=F32)
        loads[k].wait()
        out[k] = (dot(left[k], upv) + low).astype(BF16)
        c = pltpu.make_async_copy(out.at[k], err.at[0, pl.ds(k * step, step)], out_sem.at[k])
        c.start()
        stores.append(c)
    for c in stores:
        c.wait()


def on_device(activations, upstream, q_start):
    reps = lax.axis_size("rep")
    groups = lax.axis_size("fsdp")
    tok, width = activations.shape
    kvw = upstream.shape[1]
    rank = q_start.shape[1]
    rows = width // groups
    chunks = math.gcd(reps, rows // 128)
    cw = rows // chunks
    parts = 16
    cfg = (reps, groups, chunks, 4, 9, parts)
    vm = pl.BlockSpec(memory_space=pltpu.VMEM)
    hbm = pl.BlockSpec(memory_space=pl.ANY)
    dma = pltpu.SemaphoreType.DMA
    peers = groups - 1
    left_all, up_all, p_basis, q_factor = pl.pallas_call(
        functools.partial(exchange_kernel, cfg),
        out_shape=(
            jax.ShapeDtypeStruct((rows, groups * tok), BF16),
            jax.ShapeDtypeStruct((groups * tok, kvw), BF16),
            jax.ShapeDtypeStruct((rank, rows), F32),
            jax.ShapeDtypeStruct((rank, kvw), F32),
        ),
        in_specs=[hbm, vm, vm],
        out_specs=(hbm, hbm, vm, vm),
        scratch_shapes=[
            pltpu.VMEM((tok, width), BF16),
            pltpu.VMEM((width, tok), BF16),
            pltpu.VMEM((peers, rank, kvw), F32),
            pltpu.VMEM((groups, chunks, rank, cw), F32),
            pltpu.VMEM((groups * reps, rank, cw), F32),
            pltpu.VMEM((groups, chunks, rank, cw), F32),
            pltpu.VMEM((groups, rank, rows), F32),
            pltpu.VMEM((groups, rank, kvw), F32),
            pltpu.VMEM((peers, rank, kvw), F32),
            pltpu.VMEM((reps, rank, kvw), F32),
            dma((3,)),
            dma((peers,)), dma((peers,)),
            dma((peers,)), dma((peers,)),
            dma((peers, parts)), dma((peers, parts)),
            dma((groups, chunks)), dma((groups * reps,)),
            dma((groups * reps,)), dma((groups * chunks,)),
            dma((peers,)), dma((peers,)),
            dma((reps,)), dma((reps,)),
        ],
        compiler_params=pltpu.CompilerParams(collective_id=0, has_side_effects=True),
        name="exchange",
    )(activations, upstream, q_start)
    steps = 8
    step = rows // steps
    return pl.pallas_call(
        functools.partial(residual_kernel, reps),
        out_shape=(
            jax.ShapeDtypeStruct((1, rows, kvw), BF16),
            jax.ShapeDtypeStruct((1, rank, rows), F32),
            jax.ShapeDtypeStruct((1, rank, kvw), F32),
        ),
        in_specs=[hbm] * 4,
        out_specs=(hbm,) * 3,
        scratch_shapes=[
            pltpu.VMEM((steps, step, groups * tok), BF16),
            pltpu.VMEM((groups * tok, kvw), BF16),
            pltpu.VMEM((rank, rows), F32),
            pltpu.VMEM((rank, kvw), F32),
            pltpu.VMEM((steps, step, kvw), BF16),
            dma((3,)), dma((steps,)), dma((steps + 2,)),
        ],
        name="residual",
    )(left_all, up_all, p_basis, q_factor)


def solution(mesh):
    in_specs = (P(("rep", "fsdp"), None), P(("rep", "fsdp"), None), P("fsdp", None, None))
    out_specs = (P("rep", "fsdp", None), P("fsdp", None, None), P("fsdp", None, None))
    return jax.shard_map(
        on_device, mesh=mesh, in_specs=in_specs, out_specs=out_specs, check_vma=False
    )
```

time: 223 us -> 46.5 us (0.21)
  waiting for transfers between devices: 87 us -> 0 us
  blocking collectives: 61.1 us -> 0 us
  Pallas kernels: 0 us -> 45.6 us
  matrix products: 29.3 us -> 0 us
  other arithmetic: 17.4 us -> 0 us
  between operations: 16.8 us -> 0.64 us
  local copies, waits for them, and re-layouts: 6.82 us -> 0 us
  starting transfers between devices: 4.24 us -> 0 us
    psum x1 -> x0, waiting for transfers between devices: 87 us -> none  [on_device(): p_sum = lax.psum(left_local, 'rep')]
    pallas_call x0 -> x2, Pallas kernels: none -> 45.6 us  [the longest x1 40.4 us: on_device(): pl.pallas_call(functools.partial(exchange_kernel, cfg), out_shape=(jax.Sh...]
    psum x1 -> x0, blocking collectives: 32.4 us -> none  [on_device(): q_factor = lax.psum(right_local, 'rep')]
    dot_general x5 -> x0, matrix products: 29.3 us -> none  [the longest x1 11.3 us: on_device(): lax.dot_general(p_basis, q_factor / replicas, (((0,), (0,)), ((), ())), p...]
    all_gather x1 -> x0, blocking collectives: 28.7 us -> none  [on_device(): cotangent_all = lax.all_gather(upstream, 'fsdp', axis=0, tiled=True)]
    reduce_sum x7 -> x0, other arithmetic: 10.9 us -> none  [the longest x4 6.39 us: on_device(): vector = vector - jnp.sum(vector * earlier) * earlier]
    unnamed x11 -> x0, local copies, waits for them, and re-layouts: 6.82 us -> none
    div x1 -> x0, other arithmetic: 4.8 us -> none  [on_device(): basis.append(vector / jnp.sqrt(jnp.sum(vector * vector) + 1e-06))]
  transfers between devices with their start and end apart: 2 -> 0, of which waited for: 1 -> 0; matrix products, arithmetic and copies ran while one was open for 0% -> 0% of each run, Pallas kernels for 0% -> 0%
where the time goes in v2:
time: 46.5 us; the launch traced here: 46.3 us
  Pallas kernels  45.6 us (98%)
  between operations  0.64 us (1%)
    pallas_call x1, Pallas kernels, on_device(): pl.pallas_call(functools.partial(exchange_kernel, cfg), out_shape=(jax.Sh...  40.4 us
    pallas_call x1, Pallas kernels, on_device(): pl.pallas_call(functools.partial(residual_kernel, reps), out_shape=(jax.S...  5.21 us

profile of v2, /device:TPU:0, one launch (start us, length us, event | category | flops | bytes accessed | tf_op | source)
XLA Modules:
  0.0 46.3 jit_solution(16616017426583515238)
XLA Ops:
  0.6 40.4 %exchange.1 = (bf16[4096,256]{1,0:T(8,128)(2,1)}, bf16[256,512]{1,0:T(8,128)(2,1)}, f32[4,4096]{1,0:T(4,128)}, f32[4,512]{1,0:T(4,128)}) custom-call(bf16[128,8192]{1,0:T(8,128)(2,1)} %act_hbm.1, bf16[128,512]{1,0:T(8,128)(2,1)} %up.1, f32[1,4,512]{2,1,0:T(4,128)} %q0.1), custom_call_target="tpu_custom_call" | custom-call | tf_op jit(solution)/shard_map/exchange/pallas_call | solution.py:295
  41.1 5.2 %residual.1 = (bf16[1,4096,512]{2,1,0:T(8,128)(2,1)}, f32[1,4,4096]{2,1,0:T(4,128)}, f32[1,4,512]{2,1,0:T(4,128)}) custom-call(bf16[4096,256]{1,0:T(8,128)(2,1)} %get-tuple-element.7.left_hbm, bf16[256,512]{1,0:T(8,128)(2,1)} %get-tuple-element.8.up_hbm, f32[4,4096]{1,0:T(4,128)} %get-tuple-element.9.p_hbm, f32[4,512]{1,0:T(4,128)} %get-tuple-element.10.q_hbm), custom_call_target="tpu_custom_call" | custom-call | tf_op jit(solution)/shard_map/residual/pallas_call | solution.py:330

commit v3 on v2

--- a/solution.py
+++ b/solution.py
@@ -32,8 +32,8 @@
 
 
 def exchange_kernel(
-    cfg, act_hbm, up, q0, left_all, up_all, p_out, q_out,
-    act, left, q_in, pc, rs_in, pfull, p_flat, cc, c_in, g_in,
+    cfg, act_hbm, up, q0, left_all, up_all, p_out, g_in,
+    act, up_v, q_v, left, q_in, pc, rs_in, pfull, p_flat, cc, c_in, g_own,
     local_sem, q_s, q_r, u_s, u_r, b_s, b_r, rs_s, rs_r, ag_s, ag_r, c_s, c_r, g_s, g_r,
 ):
     reps, groups, chunks, part1, part2, parts = cfg
@@ -43,7 +43,7 @@
     rows = width // groups
     stride = reps // chunks
     piece = rows // parts
-    rank = q0.shape[1]
+    rank = q_v.shape[0]
     cw = rows // chunks
 
     def ahead(d):
@@ -63,6 +63,10 @@
         lax.fori_loop(a, b, body, 0)
 
     load = pltpu.make_async_copy(act_hbm, act, local_sem.at[0])
+    load_q = pltpu.make_async_copy(q0.at[0], q_v, local_sem.at[3])
+    load_up = pltpu.make_async_copy(up, up_v, local_sem.at[4])
+    load_q.start()
+    load_up.start()
     load.start()
     barrier = pltpu.get_barrier_semaphore()
     for f in range(groups):
@@ -74,9 +78,11 @@
 
         loop(0 if f else 1, reps, greet)
     my_tokens = pl.ds(pl.multiple_of(mf * tok, tok), tok)
-    keep_up = pltpu.make_async_copy(up, up_all.at[my_tokens], local_sem.at[1])
+    load_q.wait()
+    load_up.wait()
+    keep_up = pltpu.make_async_copy(up_v, up_all.at[my_tokens], local_sem.at[1])
     keep_up.start()
-    upv = up[...]
+    upv = up_v[...]
 
     def columns(g):
         return pl.ds(pl.multiple_of(g * rows, rows), rows)
@@ -92,10 +98,9 @@
         left[at, :] = act[:, at].T
 
     load.wait()
-    project(q0[0], mf)
-    loop(0, groups * parts, turn)
+    loop(0, (groups - 1) * parts, lambda i: turn(lax.rem(mf * parts + parts + i, groups * parts)))
+    project(q_v[...], mf)
     keep_left = pltpu.make_async_copy(left.at[columns(mf)], left_all.at[:, my_tokens], local_sem.at[2])
-    keep_left.start()
     pl.semaphore_wait(barrier, reps * groups - 1)
 
     qs, us, bulk, cs = [], [], [], []
@@ -124,6 +129,8 @@
             loop(0, chunks, lambda d: act_on(rs_copy(g, lax.rem(mine + d, chunks))))
 
     rs_all(mf, lambda c: c.start(), True)
+    loop(0, parts, lambda i: turn(mf * parts + i))
+    keep_left.start()
     for d in range(1, groups):
         qs[groups - d - 1].wait_recv()
         project(q_in[groups - d - 1], ahead(d))
@@ -195,29 +202,31 @@
             p_flat[g, :, c * cw:(c + 1) * cw] = v[g, c]
         t = folded(dot(two_terms(p_flat[g]), left[g * rows:(g + 1) * rows, :]))
         cc[g] = folded(dot(two_terms(t), upv))
+    keep_p = pltpu.make_async_copy(p_flat.at[mf], p_out, local_sem.at[5])
     for d in range(1, groups):
         g = ahead(d)
         cs.append(remote(me, g, cc.at[g], c_in.at[d - 1], c_s.at[d - 1], c_r.at[d - 1]))
         cs[-1].start()
     send_bulk(part2, parts)
-    p_out[...] = p_flat[mf]
+    keep_p.start()
     total = cc[mf]
     for c, got in zip(cs, range(groups - 1)):
         c.wait_recv()
         total = total + c_in[got]
-    g_in[me] = total
+    g_own[...] = total
+    keep_g = pltpu.make_async_copy(g_own, g_in.at[me], local_sem.at[6])
 
     def g_copy(i):
         j = lax.rem(me + i, reps)
-        return remote(j, mf, g_in.at[me], g_in.at[me], g_s.at[j], g_r.at[me])
+        return remote(j, mf, g_own, g_in.at[me], g_s.at[j], g_r.at[me])
 
     def g_arrive(i):
         j = lax.rem(me + i, reps)
         remote(j, mf, g_in.at[j], g_in.at[j], g_s.at[0], g_r.at[j]).wait_recv()
 
     loop(1, reps, lambda i: g_copy(i).start())
+    keep_g.start()
     loop(1, reps, g_arrive)
-    q_out[...] = jnp.sum(g_in[...], axis=0)
 
     for c in qs + cs:
         c.wait_send()
@@ -230,6 +239,8 @@
     loop(1, reps, lambda i: g_copy(i).wait_send())
     keep_up.wait()
     keep_left.wait()
+    keep_p.wait()
+    keep_g.wait()
     for c in us:
         c.wait()
     for k in range(parts):
@@ -238,12 +249,12 @@
 
 
 def residual_kernel(
-    reps, left_hbm, up_hbm, p_hbm, q_hbm, err, p_out, q_out, left, up, p, q, out, in_sem, left_sem, out_sem
+    reps, left_hbm, up_hbm, p_hbm, g_hbm, err, p_out, q_out, left, up, p, g, q, out, in_sem, left_sem, out_sem
 ):
     parts, step = left.shape[0], left.shape[1]
     small = [
         pltpu.make_async_copy(src, dst, in_sem.at[i])
-        for i, (src, dst) in enumerate(((q_hbm, q), (p_hbm, p), (up_hbm, up)))
+        for i, (src, dst) in enumerate(((g_hbm, g), (p_hbm, p), (up_hbm, up)))
     ]
     loads = [
         pltpu.make_async_copy(left_hbm.at[pl.ds(k * step, step)], left.at[k], left_sem.at[k])
@@ -253,6 +264,7 @@
         c.start()
     for c in small:
         c.wait()
+    q[...] = jnp.sum(g[...], axis=0)
     stores = [
         pltpu.make_async_copy(p, p_out.at[0], out_sem.at[parts]),
         pltpu.make_async_copy(q, q_out.at[0], out_sem.at[parts + 1]),
@@ -287,23 +299,24 @@
     chunks = math.gcd(reps, rows // 128)
     cw = rows // chunks
     parts = 16
-    cfg = (reps, groups, chunks, 4, 9, parts)
-    vm = pl.BlockSpec(memory_space=pltpu.VMEM)
+    cfg = (reps, groups, chunks, 5, 10, parts)
     hbm = pl.BlockSpec(memory_space=pl.ANY)
     dma = pltpu.SemaphoreType.DMA
     peers = groups - 1
-    left_all, up_all, p_basis, q_factor = pl.pallas_call(
+    left_all, up_all, p_basis, q_terms = pl.pallas_call(
         functools.partial(exchange_kernel, cfg),
         out_shape=(
             jax.ShapeDtypeStruct((rows, groups * tok), BF16),
             jax.ShapeDtypeStruct((groups * tok, kvw), BF16),
             jax.ShapeDtypeStruct((rank, rows), F32),
-            jax.ShapeDtypeStruct((rank, kvw), F32),
+            jax.ShapeDtypeStruct((reps, rank, kvw), F32),
         ),
-        in_specs=[hbm, vm, vm],
-        out_specs=(hbm, hbm, vm, vm),
+        in_specs=[hbm] * 3,
+        out_specs=(hbm,) * 4,
         scratch_shapes=[
             pltpu.VMEM((tok, width), BF16),
+            pltpu.VMEM((tok, kvw), BF16),
+            pltpu.VMEM((rank, kvw), F32),
             pltpu.VMEM((width, tok), BF16),
             pltpu.VMEM((peers, rank, kvw), F32),
             pltpu.VMEM((groups, chunks, rank, cw), F32),
@@ -312,8 +325,8 @@
             pltpu.VMEM((groups, rank, rows), F32),
             pltpu.VMEM((groups, rank, kvw), F32),
             pltpu.VMEM((peers, rank, kvw), F32),
-            pltpu.VMEM((reps, rank, kvw), F32),
-            dma((3,)),
+            pltpu.VMEM((rank, kvw), F32),
+            dma((7,)),
             dma((peers,)), dma((peers,)),
             dma((peers,)), dma((peers,)),
             dma((peers, parts)), dma((peers, parts)),
@@ -340,12 +353,13 @@
             pltpu.VMEM((steps, step, groups * tok), BF16),
             pltpu.VMEM((groups * tok, kvw), BF16),
             pltpu.VMEM((rank, rows), F32),
+            pltpu.VMEM((reps, rank, kvw), F32),
             pltpu.VMEM((rank, kvw), F32),
             pltpu.VMEM((steps, step, kvw), BF16),
             dma((3,)), dma((steps,)), dma((steps + 2,)),
         ],
         name="residual",
-    )(left_all, up_all, p_basis, q_factor)
+    )(left_all, up_all, p_basis, q_terms)
 
 
 def solution(mesh):

time: 46.5 us -> 45.6 us (0.981)
  Pallas kernels: 45.6 us -> 44.8 us
    pallas_call x1, Pallas kernels: 40.4 us -> 39.4 us  [on_device(): pl.pallas_call(functools.partial(exchange_kernel, cfg), out_shape=(jax.Sh...]
where the time goes in v3:
time: 45.6 us; the launch traced here: 45.4 us
  Pallas kernels  44.8 us (98%)
  between operations  0.64 us (1%)
    pallas_call x1, Pallas kernels, on_device(): pl.pallas_call(functools.partial(exchange_kernel, cfg), out_shape=(jax.Sh...  39.4 us
    pallas_call x1, Pallas kernels, on_device(): pl.pallas_call(functools.partial(residual_kernel, reps), out_shape=(jax.S...  5.31 us

profile of v3, /device:TPU:0, one launch (start us, length us, event | category | flops | bytes accessed | tf_op | source)
XLA Modules:
  0.0 45.4 jit_solution(964860587466249813)
XLA Ops:
  0.6 39.4 %exchange.1 = (bf16[4096,256]{1,0:T(8,128)(2,1)}, bf16[256,512]{1,0:T(8,128)(2,1)}, f32[4,4096]{1,0:T(4,128)}, f32[16,4,512]{2,1,0:T(4,128)}) custom-call(bf16[128,8192]{1,0:T(8,128)(2,1)} %act_hbm.1, bf16[128,512]{1,0:T(8,128)(2,1)} %up.1, f32[1,4,512]{2,1,0:T(4,128)} %q0.1), custom_call_target="tpu_custom_call" | custom-call | tf_op jit(solution)/shard_map/exchange/pallas_call | solution.py:306
  40.1 5.3 %residual.1 = (bf16[1,4096,512]{2,1,0:T(8,128)(2,1)}, f32[1,4,4096]{2,1,0:T(4,128)}, f32[1,4,512]{2,1,0:T(4,128)}) custom-call(bf16[4096,256]{1,0:T(8,128)(2,1)} %get-tuple-element.7.left_hbm, bf16[256,512]{1,0:T(8,128)(2,1)} %get-tuple-element.8.up_hbm, f32[4,4096]{1,0:T(4,128)} %get-tuple-element.9.p_hbm, f32[16,4,512]{2,1,0:T(4,128)} %get-tuple-element.10.g_hbm), custom_call_target="tpu_custom_call" | custom-call | tf_op jit(solution)/shard_map/residual/pallas_call | solution.py:343

commit v4 on v3

--- a/solution.py
+++ b/solution.py
@@ -33,8 +33,8 @@
 
 def exchange_kernel(
     cfg, act_hbm, up, q0, left_all, up_all, p_out, g_in,
-    act, up_v, q_v, left, q_in, pc, rs_in, pfull, p_flat, cc, c_in, g_own,
-    local_sem, q_s, q_r, u_s, u_r, b_s, b_r, rs_s, rs_r, ag_s, ag_r, c_s, c_r, g_s, g_r,
+    act, up_v, q_v, left, q_in, pc, rs_in, x_in, pfull, p_flat, cc, c_in, g_own,
+    local_sem, q_s, q_r, u_s, u_r, b_s, b_r, rs_s, rs_r, x_s, x_r, ag_s, ag_r, c_s, c_r, g_s, g_r,
 ):
     reps, groups, chunks, part1, part2, parts = cfg
     me = lax.axis_index("rep")
@@ -69,14 +69,12 @@
     load_up.start()
     load.start()
     barrier = pltpu.get_barrier_semaphore()
-    for f in range(groups):
-        def greet(d):
-            pl.semaphore_signal(
-                barrier, inc=1, device_id={"rep": lax.rem(me + d, reps), "fsdp": ahead(f)},
-                device_id_type=MESH,
-            )
-
-        loop(0 if f else 1, reps, greet)
+    def greet(rep, group):
+        pl.semaphore_signal(barrier, inc=1, device_id={"rep": rep, "fsdp": group}, device_id_type=MESH)
+
+    for d in range(1, groups):
+        greet(me, ahead(d))
+    loop(1, reps, lambda d: greet(lax.rem(me + d, reps), mf))
     my_tokens = pl.ds(pl.multiple_of(mf * tok, tok), tok)
     load_q.wait()
     load_up.wait()
@@ -91,7 +89,7 @@
         w = folded(dot_nt(two_terms(qv), upv))
         val = folded(dot(two_terms(w), act[:, columns(g)]))
         for c in range(chunks):
-            pc[g, c] = val[:, c * cw:(c + 1) * cw]
+            pc[c, g] = val[:, c * cw:(c + 1) * cw]
 
     def turn(i):
         at = pl.ds(pl.multiple_of(i * piece, piece), piece)
@@ -101,7 +99,7 @@
     loop(0, (groups - 1) * parts, lambda i: turn(lax.rem(mf * parts + parts + i, groups * parts)))
     project(q_v[...], mf)
     keep_left = pltpu.make_async_copy(left.at[columns(mf)], left_all.at[:, my_tokens], local_sem.at[2])
-    pl.semaphore_wait(barrier, reps * groups - 1)
+    pl.semaphore_wait(barrier, reps + groups - 2)
 
     qs, us, bulk, cs = [], [], [], []
     for d in range(1, groups):
@@ -113,28 +111,23 @@
 
     mine = me // stride
     owner = lax.rem(me, stride) == 0
-    my_slot = mf * reps + me
-
-    def rs_copy(g, c):
-        return remote(c * stride, g, pc.at[g, c], rs_in.at[my_slot], rs_s.at[g, c], rs_r.at[my_slot])
-
-    def rs_all(g, act_on, own_shard):
-        if own_shard:
-            loop(1, chunks, lambda d: act_on(rs_copy(g, lax.rem(mine + d, chunks))))
-            if stride > 1:
-                @pl.when(jnp.logical_not(owner))
-                def _():
-                    act_on(rs_copy(g, mine))
-        else:
-            loop(0, chunks, lambda d: act_on(rs_copy(g, lax.rem(mine + d, chunks))))
-
-    rs_all(mf, lambda c: c.start(), True)
+
+    def rs_copy(c):
+        return remote(c * stride, mf, pc.at[c], rs_in.at[me], rs_s.at[c], rs_r.at[me])
+
+    def rs_all(act_on):
+        loop(1, chunks, lambda d: act_on(rs_copy(lax.rem(mine + d, chunks))))
+        if stride > 1:
+            @pl.when(jnp.logical_not(owner))
+            def _():
+                act_on(rs_copy(mine))
+
     loop(0, parts, lambda i: turn(mf * parts + i))
     keep_left.start()
     for d in range(1, groups):
         qs[groups - d - 1].wait_recv()
         project(q_in[groups - d - 1], ahead(d))
-        rs_all(ahead(d), lambda c: c.start(), False)
+    rs_all(lambda c: c.start())
 
     for d in range(1, groups):
         bulk.append([
@@ -154,32 +147,41 @@
 
     send_bulk(0, part1)
 
-    def ag_copy(rep, g):
-        return remote(
-            rep, g, pfull.at[mf, mine], pfull.at[mf, mine], ag_s.at[g * reps + rep], ag_r.at[mf * chunks + mine]
-        )
+    def ag_copy(i):
+        j = lax.rem(me + i, reps)
+        return remote(j, mf, pfull.at[mine], pfull.at[mine], ag_s.at[j], ag_r.at[mine])
 
     def ag_all(act_on):
-        for d in list(range(1, groups)) + [0]:
-            loop(0 if d else 1, reps, lambda i: act_on(ag_copy(lax.rem(me + i, reps), ahead(d))))
+        loop(1, reps, lambda i: act_on(ag_copy(i)))
+
+    def across(d):
+        return remote(me, ahead(d), x_in.at[mf], x_in.at[mf], x_s.at[d - 1], x_r.at[mf])
 
     def reduce_mine():
-        rs_in[my_slot] = pc[mf, mine]
+        rs_in[me] = pc[mine]
 
         def arrive(i):
-            j = lax.rem(my_slot + i, reps * groups)
-            remote(
-                lax.rem(j, reps), j // reps, rs_in.at[j], rs_in.at[j], rs_s.at[0, 0], rs_r.at[j]
-            ).wait_recv()
-
-        loop(1, reps * groups, arrive)
-        pfull[mf, mine] = jnp.sum(rs_in[...], axis=0)
+            j = lax.rem(me + i, reps)
+            remote(j, mf, rs_in.at[j], rs_in.at[j], rs_s.at[0], rs_r.at[j]).wait_recv()
+
+        loop(1, reps, arrive)
+        x_in[mf] = jnp.sum(rs_in[...], axis=0)
+        for d in range(1, groups):
+            across(d).start()
+        for d in range(1, groups):
+            g = ahead(d)
+            remote(me, g, x_in.at[g], x_in.at[g], x_s.at[0], x_r.at[g]).wait_recv()
+        pfull[mine] = jnp.sum(x_in[...], axis=0)
         ag_all(lambda c: c.start())
 
+    def shares_done():
+        ag_all(lambda c: c.wait_send())
+        for d in range(1, groups):
+            across(d).wait_send()
+
     def gather(i):
-        j = lax.rem(mf * chunks + mine + i, groups * chunks)
-        g, c = j // chunks, lax.rem(j, chunks)
-        remote(c * stride, g, pfull.at[g, c], pfull.at[g, c], ag_s.at[0], ag_r.at[j]).wait_recv()
+        c = lax.rem(mine + i, chunks)
+        remote(c * stride, mf, pfull.at[c], pfull.at[c], ag_s.at[0], ag_r.at[c]).wait_recv()
 
     if stride > 1:
         pl.when(owner)(reduce_mine)
@@ -187,19 +189,19 @@
     else:
         reduce_mine()
     send_bulk(part1, part2)
-    loop(1, groups * chunks, gather)
+    loop(1, chunks, gather)
 
     v = pfull[...]
     row_at = lax.broadcasted_iota(jnp.int32, v.shape, 2)
     for i in range(rank):
         lead = v[:, :, i:i + 1, :]
-        dots = jnp.sum(jnp.sum(v * lead, axis=1, keepdims=True), axis=3, keepdims=True)
+        dots = jnp.sum(jnp.sum(v * lead, axis=0, keepdims=True), axis=3, keepdims=True)
         inv = lax.rsqrt(dots[:, :, i:i + 1, :] + 1e-06)
         unit = lead * inv
         v = jnp.where(row_at > i, v - (dots * inv) * unit, jnp.where(row_at == i, unit, v))
     for g in range(groups):
         for c in range(chunks):
-            p_flat[g, :, c * cw:(c + 1) * cw] = v[g, c]
+            p_flat[g, :, c * cw:(c + 1) * cw] = v[c, g]
         t = folded(dot(two_terms(p_flat[g]), left[g * rows:(g + 1) * rows, :]))
         cc[g] = folded(dot(two_terms(t), upv))
     keep_p = pltpu.make_async_copy(p_flat.at[mf], p_out, local_sem.at[5])
@@ -230,12 +232,11 @@
 
     for c in qs + cs:
         c.wait_send()
-    for d in range(groups):
-        rs_all(ahead(d), lambda c: c.wait_send(), d == 0)
+    rs_all(lambda c: c.wait_send())
     if stride > 1:
-        pl.when(owner)(lambda: ag_all(lambda c: c.wait_send()))
+        pl.when(owner)(shares_done)
     else:
-        ag_all(lambda c: c.wait_send())
+        shares_done()
     loop(1, reps, lambda i: g_copy(i).wait_send())
     keep_up.wait()
     keep_left.wait()
@@ -299,7 +300,7 @@
     chunks = math.gcd(reps, rows // 128)
     cw = rows // chunks
     parts = 16
-    cfg = (reps, groups, chunks, 5, 10, parts)
+    cfg = (reps, groups, chunks, 6, 11, parts)
     hbm = pl.BlockSpec(memory_space=pl.ANY)
     dma = pltpu.SemaphoreType.DMA
     peers = groups - 1
@@ -319,9 +320,10 @@
             pltpu.VMEM((rank, kvw), F32),
             pltpu.VMEM((width, tok), BF16),
             pltpu.VMEM((peers, rank, kvw), F32),
-            pltpu.VMEM((groups, chunks, rank, cw), F32),
-            pltpu.VMEM((groups * reps, rank, cw), F32),
-            pltpu.VMEM((groups, chunks, rank, cw), F32),
+            pltpu.VMEM((chunks, groups, rank, cw), F32),
+            pltpu.VMEM((reps, groups, rank, cw), F32),
+            pltpu.VMEM((groups, groups, rank, cw), F32),
+            pltpu.VMEM((chunks, groups, rank, cw), F32),
             pltpu.VMEM((groups, rank, rows), F32),
             pltpu.VMEM((groups, rank, kvw), F32),
             pltpu.VMEM((peers, rank, kvw), F32),
@@ -330,8 +332,9 @@
             dma((peers,)), dma((peers,)),
             dma((peers,)), dma((peers,)),
             dma((peers, parts)), dma((peers, parts)),
-            dma((groups, chunks)), dma((groups * reps,)),
-            dma((groups * reps,)), dma((groups * chunks,)),
+            dma((chunks,)), dma((reps,)),
+            dma((peers,)), dma((groups,)),
+            dma((reps,)), dma((chunks,)),
             dma((peers,)), dma((peers,)),
             dma((reps,)), dma((reps,)),
         ],

time: 45.6 us -> 42.5 us (0.932)
  Pallas kernels: 44.8 us -> 41.6 us
    pallas_call x1, Pallas kernels: 39.4 us -> 36.4 us  [on_device(): pl.pallas_call(functools.partial(exchange_kernel, cfg), out_shape=(jax.Sh...]
where the time goes in v4:
time: 42.5 us; the launch traced here: 42.3 us
  Pallas kernels  41.6 us (98%)
  between operations  0.64 us (2%)
    pallas_call x1, Pallas kernels, on_device(): pl.pallas_call(functools.partial(exchange_kernel, cfg), out_shape=(jax.Sh...  36.4 us
    pallas_call x1, Pallas kernels, on_device(): pl.pallas_call(functools.partial(residual_kernel, reps), out_shape=(jax.S...  5.26 us

profile of v4, /device:TPU:0, one launch (start us, length us, event | category | flops | bytes accessed | tf_op | source)
XLA Modules:
  0.0 42.3 jit_solution(14920382290007927316)
XLA Ops:
  0.6 36.4 %exchange.1 = (bf16[4096,256]{1,0:T(8,128)(2,1)}, bf16[256,512]{1,0:T(8,128)(2,1)}, f32[4,4096]{1,0:T(4,128)}, f32[16,4,512]{2,1,0:T(4,128)}) custom-call(bf16[128,8192]{1,0:T(8,128)(2,1)} %act_hbm.1, bf16[128,512]{1,0:T(8,128)(2,1)} %up.1, f32[1,4,512]{2,1,0:T(4,128)} %q0.1), custom_call_target="tpu_custom_call" | custom-call | tf_op jit(solution)/shard_map/exchange/pallas_call | solution.py:307
  37.0 5.3 %residual.1 = (bf16[1,4096,512]{2,1,0:T(8,128)(2,1)}, f32[1,4,4096]{2,1,0:T(4,128)}, f32[1,4,512]{2,1,0:T(4,128)}) custom-call(bf16[4096,256]{1,0:T(8,128)(2,1)} %get-tuple-element.7.left_hbm, bf16[256,512]{1,0:T(8,128)(2,1)} %get-tuple-element.8.up_hbm, f32[4,4096]{1,0:T(4,128)} %get-tuple-element.9.p_hbm, f32[16,4,512]{2,1,0:T(4,128)} %get-tuple-element.10.g_hbm), custom_call_target="tpu_custom_call" | custom-call | tf_op jit(solution)/shard_map/residual/pallas_call | solution.py:346
